TPU v7x, 32 devices: a whole 2x2x4 slice. The times are simulated.
32 devices in a mesh: slab: 8 (over z, y), sub: 4 (over x, core).
Axes of the slice: x: 2, y: 2, z: 4, core: 2. Of those that a mesh axis runs over, the one named last changes fastest.
Arguments:
- start: float32 [64, 6, 2, 16, 128], P(('slab', 'sub')), may hold values from -20 to 20
- inv_factor: bfloat16 [1024, 2, 128, 128], P(('slab', 'sub')), as said below
- partner: int32 [64, 6], P(('slab', 'sub')), may hold values from -1 to 63, as said below
- partner_face: int32 [64, 6], P(('slab', 'sub')), may hold values from -1 to 5, as said below
- elem_class: int32 [64, 16], P(('slab', 'sub')), may hold values from 0 to 3
- elem_face: int32 [64, 16], P(('slab', 'sub')), may hold values from 0 to 5
- load_map: bfloat16 [4, 2, 128, 128], replicated, may hold values from -0.375 to 0.375
- trace_map: bfloat16 [4, 2, 128, 128], replicated, may hold values from -0.25 to 0.25
Outputs:
- last_block: float32 [64, 6, 2, 16, 128], P(('slab', 'sub'))
- hessenberg: float32 [4, 5, 16, 16], replicated
Inputs may be any that keep to these rules, and one draw needn't show every extreme that they name: Global subdomain s lies on device s // 2 of the joined axes. Across faces 0 and 1 the partner lies on the same device; across face 2 on the device one lower along sub, face 3 one higher along sub, face 4 one lower along slab, face 5 one higher along slab, and -1 exactly where no such device exists. `partner_face`: faces 0 and 1 meet face 0 or 1 of their partner; faces 2, 3, 4, 5 meet faces 3, 2, 5, 4; -1 exactly where partner is -1. `inv_factor`: each factor is lower triangular with a real diagonal of 0.5 to 2 and a small imaginary diagonal.
All inputs are finite; a program needn't handle non-finite values.
Results may differ from a plain program's by a relative error of at most 0.013.
Values sent between devices are 32-bit elements; how exact they have to be, the bound alone decides.
No kernel may reach another device: no remote copies, remote signals or barrier semaphores. Data moves between devices by JAX's collectives and lax.ppermute only.
A program may use at most 64 MiB of HBM per device.

v0:
```python
import jax
import jax.numpy as jnp
from jax import lax
from jax.sharding import PartitionSpec as P

ITERS = 4
HIGHEST_PRECISION = lax.Precision.HIGHEST


def extended(x, sides, width):
    for axis, dim in sides:
        count, length = (lax.axis_size(axis), x.shape[dim])
        up = [(i, (i + 1) % count) for i in range(count - 1)]
        down = [(j, i) for i, j in up]
        last = lax.slice_in_dim(x, length - width, length, axis=dim)
        leading = lax.slice_in_dim(x, 0, width, axis=dim)
        before = lax.ppermute(last, axis, up)
        after = lax.ppermute(leading, axis, down)
        x = jnp.concatenate([before, x, after], axis=dim)
    return x


def complex_apply(layout, matrix_real, matrix_imag, vec_real, vec_imag):
    real_part = jnp.einsum(
        layout, matrix_real, vec_real, preferred_element_type=jnp.float32
    ) - jnp.einsum(layout, matrix_imag, vec_imag, preferred_element_type=jnp.float32)
    imag_part = jnp.einsum(
        layout, matrix_real, vec_imag, preferred_element_type=jnp.float32
    ) + jnp.einsum(layout, matrix_imag, vec_real, preferred_element_type=jnp.float32)
    return (real_part, imag_part)


def factor_apply(inv_factor, vector_b, adjoint):
    factor_real = inv_factor[:, 0]
    factor_imag = inv_factor[:, 1]
    vec_real = vector_b[:, 0]
    vec_imag = vector_b[:, 1]
    if adjoint:
        layout = "eji,erj->eri"
        real_part = jnp.einsum(
            layout, factor_real, vec_real, preferred_element_type=jnp.float32
        ) + jnp.einsum(layout, factor_imag, vec_imag, preferred_element_type=jnp.float32)
        imag_part = jnp.einsum(
            layout, factor_real, vec_imag, preferred_element_type=jnp.float32
        ) - jnp.einsum(layout, factor_imag, vec_real, preferred_element_type=jnp.float32)
    else:
        layout = "eij,erj->eri"
        real_part, imag_part = complex_apply(layout, factor_real, factor_imag, vec_real, vec_imag)
    return jnp.stack([real_part, imag_part], axis=1)


def partner_traces(outgoing, partner, partner_face):
    sub_count = outgoing.shape[0]
    has_partner = partner >= 0
    local_index = jnp.where(has_partner, partner % sub_count, 0)
    face_index = jnp.where(has_partner, partner_face, 0)
    beside_all = extended(outgoing[None, None], (("slab", 0), ("sub", 1)), 1)
    trace_pool = beside_all.reshape((9 * sub_count * 6,) + outgoing.shape[2:])
    block_table = jnp.array([4, 4, 3, 5, 1, 7], jnp.int32)
    source_slot = (block_table[None, :] * sub_count + local_index) * 6 + face_index
    picked = trace_pool[source_slot]
    return jnp.where(has_partner[:, :, None, None, None], picked, 0.0)


def apply_operator(
    vector, inv_factor, partner, partner_face, elem_class, elem_face, load_map, trace_map
):
    sub_count = vector.shape[0]
    elem_count = elem_class.shape[1]
    rhs_count = vector.shape[3]
    wave_count = load_map.shape[2]
    vector_b = vector.astype(jnp.bfloat16)
    elem_load_map = load_map[elem_class]
    elem_trace_map = trace_map[elem_class]
    face_traces = jnp.take_along_axis(vector_b, elem_face[:, :, None, None, None], axis=1)
    load_real, load_imag = complex_apply(
        "sepq,serq->serp",
        elem_load_map[:, :, 0],
        elem_load_map[:, :, 1],
        face_traces[:, :, 0],
        face_traces[:, :, 1],
    )
    chosen_b = (
        jnp.stack([load_real, load_imag], axis=2)
        .astype(jnp.bfloat16)
        .reshape(sub_count * elem_count, 2, rhs_count, wave_count)
    )
    middle = factor_apply(inv_factor, chosen_b, False).astype(jnp.bfloat16)
    coefficients = (
        factor_apply(inv_factor, middle, True)
        .astype(jnp.bfloat16)
        .reshape(sub_count, elem_count, 2, rhs_count, wave_count)
    )
    trace_real, trace_imag = complex_apply(
        "seqp,serp->serq",
        elem_trace_map[:, :, 0],
        elem_trace_map[:, :, 1],
        coefficients[:, :, 0],
        coefficients[:, :, 1],
    )
    accumulated = jnp.stack([trace_real, trace_imag], axis=2)
    face_onehot = (elem_face[:, :, None] == jnp.arange(6, dtype=jnp.int32)[None, None, :]).astype(
        jnp.float32
    )
    outgoing = (
        jnp.einsum("sef,sexrq->sfxrq", face_onehot, accumulated, precision=HIGHEST_PRECISION)
        - vector
    )
    return vector - partner_traces(outgoing, partner, partner_face)


def local_inner(left, right):
    return jnp.einsum("sfxiq,sfxjq->ij", left, right, precision=HIGHEST_PRECISION)


def normalize(vector, gram_matrix):
    low_factor = jnp.linalg.cholesky(gram_matrix)
    identity = jnp.eye(gram_matrix.shape[0], dtype=jnp.float32)
    inverse = lax.linalg.triangular_solve(low_factor, identity, left_side=True, lower=True)
    return (
        jnp.einsum("sfxaq,ba->sfxbq", vector, inverse, precision=HIGHEST_PRECISION),
        low_factor.T,
    )


def body(start, inv_factor, partner, partner_face, elem_class, elem_face, load_map, trace_map):
    rhs_count = start.shape[3]
    entry_count = start.size // rhs_count * lax.axis_size("slab") * lax.axis_size("sub")
    start_gram = lax.psum(local_inner(start, start), ("slab", "sub")) / entry_count
    basis_block, upper_factor = normalize(start, start_gram)
    blocks = [basis_block]
    hessenberg = jnp.zeros((ITERS, ITERS + 1, rhs_count, rhs_count), jnp.float32)
    for number in range(ITERS):
        image_block = apply_operator(
            blocks[-1],
            inv_factor,
            partner,
            partner_face,
            elem_class,
            elem_face,
            load_map,
            trace_map,
        )
        stacked = jnp.stack(blocks)
        local_terms = jnp.einsum(
            "ksfxiq,sfxjq->kij", stacked, image_block, precision=HIGHEST_PRECISION
        )
        summed_terms, raw_gram = lax.psum(
            (local_terms, local_inner(image_block, image_block)), ("slab", "sub")
        )
        projection = summed_terms / entry_count
        image_block = image_block - jnp.einsum(
            "ksfxaq,kab->sfxbq", stacked, projection, precision=HIGHEST_PRECISION
        )
        gram_matrix = raw_gram / entry_count - jnp.einsum(
            "kai,kaj->ij", projection, projection, precision=HIGHEST_PRECISION
        )
        basis_block, upper_factor = normalize(image_block, gram_matrix)
        hessenberg = hessenberg.at[number, : number + 1].set(projection)
        hessenberg = hessenberg.at[number, number + 1].set(upper_factor)
        blocks.append(basis_block)
    return (blocks[-1], hessenberg)


def solution(mesh):
    placed = (
        P(("slab", "sub"), None, None, None, None),
        P(("slab", "sub"), None, None, None),
        P(("slab", "sub"), None),
        P(("slab", "sub"), None),
        P(("slab", "sub"), None),
        P(("slab", "sub"), None),
        P(),
        P(),
    )
    return jax.shard_map(
        body,
        mesh=mesh,
        in_specs=placed,
        out_specs=(P(("slab", "sub"), None, None, None, None), P()),
        check_vma=False,
    )
```

profile of v0, /device:TPU:0, one launch (start us, length us, event | category | flops | bytes accessed | tf_op | source)
XLA Modules:
  0.0 421.1 jit_solution(14362382191184048011)
XLA Ops:
  2.8 2.1 gather_fusion
  5.0 1.9 copy.19
  7.2 42.0 %psum.63 = f32[16,16]{0,1:T(8,128)S(1)} all-reduce(f32[16,16]{0,1:T(8,128)S(1)} %convolution_bitcast_fusion.21), channel_id=1, replica_groups=mesh['slab'=8,'sub'=4] {'slab','sub'}, use_global_device_ids=true, to_apply=%region_0.0 | all-reduce | flops 256 | bytes 2048 | tf_op jit(solution)/shard_map/psum | solution.py:129
  49.3 1.5 cholesky.89
  55.4 2.0 fusion.119
  57.4 1.9 fusion.13
  59.3 1.9 fusion.12
  65.1 2.1 gather_fusion.1
  67.2 1.7 copy.22
  73.9 4.8 %collective-permute-start = (f32[1,1,2,6,2,16,128]{6,5,4,3,2,1,0:T(8,128)S(1)}, f32[1,1,2,6,2,16,128]{6,5,4,3,2,1,0:T(8,128)S(1)}, u32[]{:S(2)}, u32[]{:S(2)}) collective-permute-start(f32[1,1,2,6,2,16,128]{6,5,4,3,2,1,0:T(8,128)S(1)} %fusion.108), channel_id=1, source_target_pairs={{0,4},{4,8},{8,12},{12,16},{16,20},{20,24},{24,28},{1,5},{5,9},{9,... | collective-permute-start | bytes 589832 | tf_op jit(solution)/shard_map/ppermute | solution.py:17
  78.7 1.7 collective-permute-done.1
  80.4 3.9 collective-permute-done
  86.4 3.9 collective-permute-start.2
  91.4 2.7 pad_maximum_fusion
  94.2 2.0 gather_fusion.2
  97.0 48.7 %all-reduce.4 = (f32[16,16]{0,1:T(8,128)S(1)}, f32[1,16,16]{2,1,0:T(8,128)S(1)}) all-reduce(f32[16,16]{0,1:T(8,128)S(1)} %convolution_bitcast_fusion.20, f32[1,16,16]{2,1,0:T(8,128)S(1)} %convolution_bitcast_fusion.19), channel_id=1, replica_groups=mesh['slab'=8,'sub'=4] {'slab','sub'}, use_global_device_ids=true, to_apply=%region_3.7 | all-reduce | flops 512 | bytes 4096 | tf_op jit(solution)/shard_map/psum | solution.py:148
  146.3 1.5 cholesky.100
  152.2 2.0 fusion.116
  154.2 1.9 fusion.117
  165.0 1.3 collective-permute-start.5
  166.3 4.8 %collective-permute-start.4 = (f32[1,1,2,6,2,16,128]{6,5,4,3,2,1,0:T(8,128)S(1)}, f32[1,1,2,6,2,16,128]{6,5,4,3,2,1,0:T(8,128)S(1)}, u32[]{:S(2)}, u32[]{:S(2)}) collective-permute-start(f32[1,1,2,6,2,16,128]{6,5,4,3,2,1,0:T(8,128)S(1)} %fusion.103), channel_id=1, source_target_pairs={{0,4},{4,8},{8,12},{12,16},{16,20},{20,24},{24,28},{1,5},{5,9},{9,... | collective-permute-start | bytes 589832 | tf_op jit(solution)/shard_map/ppermute | solution.py:17
  171.2 1.7 collective-permute-done.5
  172.9 3.8 collective-permute-done.4
  176.8 1.3 collective-permute-start.7
  178.1 3.1 collective-permute-start.6
  181.1 1.6 collective-permute-done.6
  182.7 1.4 pad_maximum_fusion.1
  184.1 2.0 gather_fusion.3
  187.1 47.8 %all-reduce.3 = (f32[2,16,16]{2,1,0:T(8,128)S(1)}, f32[16,16]{0,1:T(8,128)S(1)}) all-reduce(f32[2,16,16]{2,1,0:T(8,128)S(1)} %convolution_bitcast_fusion.7, f32[16,16]{0,1:T(8,128)S(1)} %convolution_bitcast_fusion.18), channel_id=1, replica_groups=mesh['slab'=8,'sub'=4] {'slab','sub'}, use_global_device_ids=true, to_apply=%region_6.10 | all-reduce | flops 768 | bytes 6144 | tf_op jit(solution)/shard_map/psum | solution.py:148
  235.5 1.5 cholesky.111
  241.4 2.0 fusion.114
  243.4 1.9 fusion.115
  255.5 4.9 %collective-permute-start.8 = (f32[1,1,2,6,2,16,128]{6,5,4,3,2,1,0:T(8,128)S(1)}, f32[1,1,2,6,2,16,128]{6,5,4,3,2,1,0:T(8,128)S(1)}, u32[]{:S(2)}, u32[]{:S(2)}) collective-permute-start(f32[1,1,2,6,2,16,128]{6,5,4,3,2,1,0:T(8,128)S(1)} %fusion.101), channel_id=1, source_target_pairs={{0,4},{4,8},{8,12},{12,16},{16,20},{20,24},{24,28},{1,5},{5,9},{9,... | collective-permute-start | bytes 589832 | tf_op jit(solution)/shard_map/ppermute | solution.py:17
  260.4 1.7 collective-permute-done.9
  262.1 3.9 collective-permute-done.8
  267.3 3.1 collective-permute-start.10
  271.9 1.4 pad_maximum_fusion.2
  273.3 2.0 gather_fusion.4
  276.5 49.0 %all-reduce.2 = (f32[3,16,16]{2,1,0:T(8,128)S(1)}, f32[16,16]{0,1:T(8,128)S(1)}) all-reduce(f32[3,16,16]{2,1,0:T(8,128)S(1)} %convolution_bitcast_fusion.6, f32[16,16]{0,1:T(8,128)S(1)} %convolution_bitcast_fusion.17), channel_id=1, replica_groups=mesh['slab'=8,'sub'=4] {'slab','sub'}, use_global_device_ids=true, to_apply=%region_8.12 | all-reduce | flops 1024 | bytes 8192 | tf_op jit(solution)/shard_map/psum | solution.py:148
  326.3 1.5 cholesky.122
  332.2 2.0 fusion.112
  334.2 1.9 fusion.113
  346.3 4.8 %collective-permute-start.12 = (f32[1,1,2,6,2,16,128]{6,5,4,3,2,1,0:T(8,128)S(1)}, f32[1,1,2,6,2,16,128]{6,5,4,3,2,1,0:T(8,128)S(1)}, u32[]{:S(2)}, u32[]{:S(2)}) collective-permute-start(f32[1,1,2,6,2,16,128]{6,5,4,3,2,1,0:T(8,128)S(1)} %fusion.99), channel_id=1, source_target_pairs={{0,4},{4,8},{8,12},{12,16},{16,20},{20,24},{24,28},{1,5},{5,9},{9,... | collective-permute-start | bytes 589832 | tf_op jit(solution)/shard_map/ppermute | solution.py:17
  352.8 3.7 collective-permute-done.12
  357.9 3.8 collective-permute-start.14
  363.3 1.4 pad_maximum_fusion.3
  366.6 47.3 %all-reduce.1 = (f32[4,16,16]{2,1,0:T(8,128)S(1)}, f32[16,16]{0,1:T(8,128)S(1)}) all-reduce(f32[4,16,16]{2,1,0:T(8,128)S(1)} %convolution_bitcast_fusion.5, f32[16,16]{0,1:T(8,128)S(1)} %convolution_bitcast_fusion.16), channel_id=1, replica_groups=mesh['slab'=8,'sub'=4] {'slab','sub'}, use_global_device_ids=true, to_apply=%region_10.14 | all-reduce | flops 1280 | bytes 10240 | tf_op jit(solution)/shard_map/psum | solution.py:148
  414.6 1.5 cholesky.133
  (235 shorter events, 81.7 us)
Async XLA Ops:
  0.6 2.2 copy-start
  5.0 1.9 copy-start.11
  6.9 47.9 %copy-start.2 = (bf16[32,2,128,128]{3,2,0,1:T(8,128)(2,1)}, bf16[32,2,128,128]{3,2,0,1:T(8,128)(2,1)S(1)}, u32[]{:S(2)}) copy-start(bf16[32,2,128,128]{3,2,0,1:T(8,128)(2,1)S(1)} %copy.19) | copy-start | bytes 6291460
  55.4 5.8 %copy-start.1 = (bf16[32,2,128,128]{3,2,1,0:T(8,128)(2,1)S(1)}, bf16[32,2,128,128]{3,2,1,0:T(8,128)(2,1)}, u32[]{:S(2)}) copy-start(bf16[32,2,128,128]{3,2,1,0:T(8,128)(2,1)} %param.34) | copy-start | bytes 6291460
  63.6 1.5 copy-start.10
  69.0 2.4 copy-start.6
  70.7 1.4 copy-start.21
  72.0 18.3 %copy-start.24 = (s32[2,6]{1,0:T(2,128)S(1)}, s32[2,6]{1,0:T(2,128)}, u32[]{:S(2)}) copy-start(s32[2,6]{1,0:T(2,128)} %param.36) | copy-start | bytes 148
  72.0 18.3 %copy-start.25 = (s32[2,6]{1,0:T(2,128)S(1)}, s32[2,6]{1,0:T(2,128)}, u32[]{:S(2)}) copy-start(s32[2,6]{1,0:T(2,128)} %param.35) | copy-start | bytes 148
  72.0 18.3 %copy-start.26 = (s32[6]{0:T(128)S(1)}, s32[6]{0:T(128)}, u32[]{:S(2)}) copy-start(s32[6]{0:T(128)} %constant.343) | copy-start | bytes 76
  72.6 7.8 %collective-permute-start.1 = (f32[1,1,2,6,2,16,128]{6,5,4,3,2,1,0:T(8,128)S(1)}, f32[1,1,2,6,2,16,128]{6,5,4,3,2,1,0:T(8,128)S(1)}, u32[]{:S(2)}, u32[]{:S(2)}) collective-permute-start(f32[1,1,2,6,2,16,128]{6,5,4,3,2,1,0:T(8,128)S(1)} %fusion.108), channel_id=1, source_target_pairs={{4,0},{8,4},{12,8},{16,12},{20,16},{24,20},{28,24},{5,1},{9,5},{13... | collective-permute-start | bytes 589832 | tf_op jit(solution)/shard_map/ppermute | solution.py:18
  73.9 10.4 %collective-permute-start = (f32[1,1,2,6,2,16,128]{6,5,4,3,2,1,0:T(8,128)S(1)}, f32[1,1,2,6,2,16,128]{6,5,4,3,2,1,0:T(8,128)S(1)}, u32[]{:S(2)}, u32[]{:S(2)}) collective-permute-start(f32[1,1,2,6,2,16,128]{6,5,4,3,2,1,0:T(8,128)S(1)} %fusion.108), channel_id=1, source_target_pairs={{0,4},{4,8},{8,12},{12,16},{16,20},{20,24},{24,28},{1,5},{5,9},{9,... | collective-permute-start | bytes 589832 | tf_op jit(solution)/shard_map/ppermute | solution.py:17
  85.2 5.3 %collective-permute-start.3 = (f32[3,1,2,6,2,16,128]{6,5,4,3,2,1,0:T(8,128)}, f32[3,1,2,6,2,16,128]{6,5,4,3,2,1,0:T(8,128)}, u32[]{:S(2)}, u32[]{:S(2)}) collective-permute-start(f32[3,1,2,6,2,16,128]{6,5,4,3,2,1,0:T(8,128)} %pad_maximum_fusion.5), channel_id=1, source_target_pairs={{1,0},{2,1},{3,2},{5,4},{6,5},{7,6},{9,8},{10,9},{11,10},{13,12},{... | collective-permute-start | bytes 1769480 | tf_op jit(solution)/shard_map/ppermute | solution.py:18
  86.4 5.0 %collective-permute-start.2 = (f32[3,1,2,6,2,16,128]{6,5,4,3,2,1,0:T(8,128)}, f32[3,1,2,6,2,16,128]{6,5,4,3,2,1,0:T(8,128)}, u32[]{:S(2)}, u32[]{:S(2)}) collective-permute-start(f32[3,1,2,6,2,16,128]{6,5,4,3,2,1,0:T(8,128)} %pad_maximum_fusion.5), channel_id=1, source_target_pairs={{0,1},{1,2},{2,3},{4,5},{5,6},{6,7},{8,9},{9,10},{10,11},{12,13},{... | collective-permute-start | bytes 1769480 | tf_op jit(solution)/shard_map/ppermute | solution.py:17
  90.4 184.9 %copy-start.22 = (pred[2,6]{1,0:T(4,128)(4,1)}, pred[2,6]{1,0:T(4,128)(4,1)S(1)}, u32[]{:S(2)}) copy-start(pred[2,6]{1,0:T(4,128)(4,1)S(1)} %broadcast_compare_fusion) | copy-start | bytes 40
  152.1 4.0 copy-start.3
  159.8 1.6 copy-start.7
  165.0 7.9 %collective-permute-start.5 = (f32[1,1,2,6,2,16,128]{6,5,4,3,2,1,0:T(8,128)S(1)}, f32[1,1,2,6,2,16,128]{6,5,4,3,2,1,0:T(8,128)S(1)}, u32[]{:S(2)}, u32[]{:S(2)}) collective-permute-start(f32[1,1,2,6,2,16,128]{6,5,4,3,2,1,0:T(8,128)S(1)} %fusion.103), channel_id=1, source_target_pairs={{4,0},{8,4},{12,8},{16,12},{20,16},{24,20},{28,24},{5,1},{9,5},{13... | collective-permute-start | bytes 589832 | tf_op jit(solution)/shard_map/ppermute | solution.py:18
  166.3 10.4 %collective-permute-start.4 = (f32[1,1,2,6,2,16,128]{6,5,4,3,2,1,0:T(8,128)S(1)}, f32[1,1,2,6,2,16,128]{6,5,4,3,2,1,0:T(8,128)S(1)}, u32[]{:S(2)}, u32[]{:S(2)}) collective-permute-start(f32[1,1,2,6,2,16,128]{6,5,4,3,2,1,0:T(8,128)S(1)} %fusion.103), channel_id=1, source_target_pairs={{0,4},{4,8},{8,12},{12,16},{16,20},{20,24},{24,28},{1,5},{5,9},{9,... | collective-permute-start | bytes 589832 | tf_op jit(solution)/shard_map/ppermute | solution.py:17
  176.8 4.4 %collective-permute-start.7 = (f32[3,1,2,6,2,16,128]{6,5,4,3,2,1,0:T(8,128)S(1)}, f32[3,1,2,6,2,16,128]{6,5,4,3,2,1,0:T(8,128)S(1)}, u32[]{:S(2)}, u32[]{:S(2)}) collective-permute-start(f32[3,1,2,6,2,16,128]{6,5,4,3,2,1,0:T(8,128)S(1)} %pad_maximum_fusion.6), channel_id=1, source_target_pairs={{1,0},{2,1},{3,2},{5,4},{6,5},{7,6},{9,8},{10,9},{11,10},{13,12},{... | collective-permute-start | bytes 1769480 | tf_op jit(solution)/shard_map/ppermute | solution.py:18
  178.1 4.7 %collective-permute-start.6 = (f32[3,1,2,6,2,16,128]{6,5,4,3,2,1,0:T(8,128)S(1)}, f32[3,1,2,6,2,16,128]{6,5,4,3,2,1,0:T(8,128)S(1)}, u32[]{:S(2)}, u32[]{:S(2)}) collective-permute-start(f32[3,1,2,6,2,16,128]{6,5,4,3,2,1,0:T(8,128)S(1)} %pad_maximum_fusion.6), channel_id=1, source_target_pairs={{0,1},{1,2},{2,3},{4,5},{5,6},{6,7},{8,9},{9,10},{10,11},{12,13},{... | collective-permute-start | bytes 1769480 | tf_op jit(solution)/shard_map/ppermute | solution.py:17
  234.8 5.3 %copy-start.16 = (f32[2,16,16]{2,1,0:T(8,128)}, f32[2,16,16]{2,1,0:T(8,128)S(1)}, u32[]{:S(2)}) copy-start(f32[2,16,16]{2,1,0:T(8,128)S(1)} %get-tuple-element.105) | copy-start | bytes 6148
  241.3 4.0 copy-start.4
  249.0 1.6 copy-start.8
  254.2 7.9 %collective-permute-start.9 = (f32[1,1,2,6,2,16,128]{6,5,4,3,2,1,0:T(8,128)S(1)}, f32[1,1,2,6,2,16,128]{6,5,4,3,2,1,0:T(8,128)S(1)}, u32[]{:S(2)}, u32[]{:S(2)}) collective-permute-start(f32[1,1,2,6,2,16,128]{6,5,4,3,2,1,0:T(8,128)S(1)} %fusion.101), channel_id=1, source_target_pairs={{4,0},{8,4},{12,8},{16,12},{20,16},{24,20},{28,24},{5,1},{9,5},{13... | collective-permute-start | bytes 589832 | tf_op jit(solution)/shard_map/ppermute | solution.py:18
  255.5 10.4 %collective-permute-start.8 = (f32[1,1,2,6,2,16,128]{6,5,4,3,2,1,0:T(8,128)S(1)}, f32[1,1,2,6,2,16,128]{6,5,4,3,2,1,0:T(8,128)S(1)}, u32[]{:S(2)}, u32[]{:S(2)}) collective-permute-start(f32[1,1,2,6,2,16,128]{6,5,4,3,2,1,0:T(8,128)S(1)} %fusion.101), channel_id=1, source_target_pairs={{0,4},{4,8},{8,12},{12,16},{16,20},{20,24},{24,28},{1,5},{5,9},{9,... | collective-permute-start | bytes 589832 | tf_op jit(solution)/shard_map/ppermute | solution.py:17
  266.0 5.0 %collective-permute-start.11 = (f32[3,1,2,6,2,16,128]{6,5,4,3,2,1,0:T(8,128)S(1)}, f32[3,1,2,6,2,16,128]{6,5,4,3,2,1,0:T(8,128)S(1)}, u32[]{:S(2)}, u32[]{:S(2)}) collective-permute-start(f32[3,1,2,6,2,16,128]{6,5,4,3,2,1,0:T(8,128)S(1)} %pad_maximum_fusion.7), channel_id=1, source_target_pairs={{1,0},{2,1},{3,2},{5,4},{6,5},{7,6},{9,8},{10,9},{11,10},{13,12},{... | collective-permute-start | bytes 1769480 | tf_op jit(solution)/shard_map/ppermute | solution.py:18
  267.3 4.7 %collective-permute-start.10 = (f32[3,1,2,6,2,16,128]{6,5,4,3,2,1,0:T(8,128)S(1)}, f32[3,1,2,6,2,16,128]{6,5,4,3,2,1,0:T(8,128)S(1)}, u32[]{:S(2)}, u32[]{:S(2)}) collective-permute-start(f32[3,1,2,6,2,16,128]{6,5,4,3,2,1,0:T(8,128)S(1)} %pad_maximum_fusion.7), channel_id=1, source_target_pairs={{0,1},{1,2},{2,3},{4,5},{5,6},{6,7},{8,9},{9,10},{10,11},{12,13},{... | collective-permute-start | bytes 1769480 | tf_op jit(solution)/shard_map/ppermute | solution.py:17
  325.5 5.4 %copy-start.14 = (f32[3,16,16]{2,1,0:T(8,128)}, f32[3,16,16]{2,1,0:T(8,128)S(1)}, u32[]{:S(2)}) copy-start(f32[3,16,16]{2,1,0:T(8,128)S(1)} %get-tuple-element.103) | copy-start | bytes 9220
  332.1 4.0 copy-start.5
  339.8 1.6 copy-start.9
  343.8 7.4 %copy-start.18 = (f32[1,1,16,16]{2,3,1,0:T(8,128)S(1)}, f32[1,1,16,16]{2,3,1,0:T(8,128)}, u32[]{:S(2)}) copy-start(f32[1,1,16,16]{2,3,1,0:T(8,128)} %get-tuple-element.115) | copy-start | bytes 3076
  343.8 8.7 %copy-start.19 = (f32[1,1,16,16]{2,3,1,0:T(8,128)S(1)}, f32[1,1,16,16]{2,3,1,0:T(8,128)}, u32[]{:S(2)}) copy-start(f32[1,1,16,16]{2,3,1,0:T(8,128)} %get-tuple-element.113) | copy-start | bytes 3076
  344.4 17.3 %copy-start.17 = (f32[2,16,16]{2,1,0:T(8,128)S(1)}, f32[2,16,16]{2,1,0:T(8,128)}, u32[]{:S(2)}) copy-start(f32[2,16,16]{2,1,0:T(8,128)} %copy-done.16) | copy-start | bytes 6148
  344.4 17.3 %copy-start.20 = (f32[1,1,16,16]{2,3,1,0:T(8,128)S(1)}, f32[1,1,16,16]{2,3,1,0:T(8,128)}, u32[]{:S(2)}) copy-start(f32[1,1,16,16]{2,3,1,0:T(8,128)} %get-tuple-element.111) | copy-start | bytes 3076
  344.4 17.4 %copy-start.15 = (f32[3,16,16]{2,1,0:T(8,128)S(1)}, f32[3,16,16]{2,1,0:T(8,128)}, u32[]{:S(2)}) copy-start(f32[3,16,16]{2,1,0:T(8,128)} %copy-done.14) | copy-start | bytes 9220
  345.0 7.8 %collective-permute-start.13 = (f32[1,1,2,6,2,16,128]{6,5,4,3,2,1,0:T(8,128)S(1)}, f32[1,1,2,6,2,16,128]{6,5,4,3,2,1,0:T(8,128)S(1)}, u32[]{:S(2)}, u32[]{:S(2)}) collective-permute-start(f32[1,1,2,6,2,16,128]{6,5,4,3,2,1,0:T(8,128)S(1)} %fusion.99), channel_id=1, source_target_pairs={{4,0},{8,4},{12,8},{16,12},{20,16},{24,20},{28,24},{5,1},{9,5},{13... | collective-permute-start | bytes 589832 | tf_op jit(solution)/shard_map/ppermute | solution.py:18
  346.3 10.2 %collective-permute-start.12 = (f32[1,1,2,6,2,16,128]{6,5,4,3,2,1,0:T(8,128)S(1)}, f32[1,1,2,6,2,16,128]{6,5,4,3,2,1,0:T(8,128)S(1)}, u32[]{:S(2)}, u32[]{:S(2)}) collective-permute-start(f32[1,1,2,6,2,16,128]{6,5,4,3,2,1,0:T(8,128)S(1)} %fusion.99), channel_id=1, source_target_pairs={{0,4},{4,8},{8,12},{12,16},{16,20},{20,24},{24,28},{1,5},{5,9},{9,... | collective-permute-start | bytes 589832 | tf_op jit(solution)/shard_map/ppermute | solution.py:17
  356.5 8.8 %copy-start.23 = (pred[2,6]{1,0:T(4,128)(4,1)S(1)}, pred[2,6]{1,0:T(4,128)(4,1)}, u32[]{:S(2)}) copy-start(pred[2,6]{1,0:T(4,128)(4,1)} %copy-done.22) | copy-start | bytes 40
  356.6 5.3 %collective-permute-start.15 = (f32[3,1,2,6,2,16,128]{6,5,4,3,2,1,0:T(8,128)S(1)}, f32[3,1,2,6,2,16,128]{6,5,4,3,2,1,0:T(8,128)S(1)}, u32[]{:S(2)}, u32[]{:S(2)}) collective-permute-start(f32[3,1,2,6,2,16,128]{6,5,4,3,2,1,0:T(8,128)S(1)} %pad_maximum_fusion.9), channel_id=1, source_target_pairs={{1,0},{2,1},{3,2},{5,4},{6,5},{7,6},{9,8},{10,9},{11,10},{13,12},{... | collective-permute-start | bytes 1769480 | tf_op jit(solution)/shard_map/ppermute | solution.py:18
  357.9 5.4 %collective-permute-start.14 = (f32[3,1,2,6,2,16,128]{6,5,4,3,2,1,0:T(8,128)S(1)}, f32[3,1,2,6,2,16,128]{6,5,4,3,2,1,0:T(8,128)}, u32[]{:S(2)}, u32[]{:S(2)}) collective-permute-start(f32[3,1,2,6,2,16,128]{6,5,4,3,2,1,0:T(8,128)S(1)} %pad_maximum_fusion.9), channel_id=1, source_target_pairs={{0,1},{1,2},{2,3},{4,5},{5,6},{6,7},{8,9},{9,10},{10,11},{12,13},{... | collective-permute-start | bytes 1769480 | tf_op jit(solution)/shard_map/ppermute | solution.py:17
  361.8 0.7 copy-start.13
  362.5 0.8 copy-start.12
where the time goes:
time: 423 us; the launch traced here: 421 us
  blocking collectives  235 us (56%)
  matrix products  61.2 us (14%)
  starting transfers between devices  43.5 us (10%)
  other arithmetic  33.8 us (8%)
  waiting for transfers between devices  24.1 us (6%)
  local copies, waits for them, and re-layouts  22.5 us (5%)
    psum x4, blocking collectives, body(): lax.psum((local_terms, local_inner(image_block, image_block)), ('slab', '...  193 us
    psum x1, blocking collectives, body(): lax.psum(local_inner(start, start), ('slab', 'sub')) / entry_count  42 us
    ppermute x8, starting transfers between devices, extended(): before = lax.ppermute(last, axis, up)  33.2 us
    ppermute x8, waiting for transfers between devices, extended(): before = lax.ppermute(last, axis, up)  18.7 us
    dot_general x12, matrix products, complex_apply(): jnp.einsum(layout, matrix_real, vec_real, preferred_element_type=jnp.floa...  12.9 us
    dot_general x12, matrix products, complex_apply(): jnp.einsum(layout, matrix_real, vec_imag, preferred_element_type=jnp.floa...  11.8 us
    another operation x15, other arithmetic, normalize(): low_factor = jnp.linalg.cholesky(gram_matrix)  10.7 us
    ppermute x8, starting transfers between devices, extended(): after = lax.ppermute(leading, axis, down)  10.3 us
  transfers between devices with their start and end apart: 16, of which 11 were waited for; matrix products, arithmetic and copies ran while one was open for 1% of the time, Pallas kernels for 0%

commit v1 on v0

--- a/solution.py
+++ b/solution.py
@@ -5,6 +5,12 @@
 
 ITERS = 4
 HIGHEST_PRECISION = lax.Precision.HIGHEST
+
+
+def add_all(x, axis):
+    pieces = lax.all_gather(x, axis, axis=0, tiled=False)
+    total = pieces.sum(axis=0)
+    return total
 
 
 def extended(x, sides, width):
@@ -126,7 +132,7 @@
 def body(start, inv_factor, partner, partner_face, elem_class, elem_face, load_map, trace_map):
     rhs_count = start.shape[3]
     entry_count = start.size // rhs_count * lax.axis_size("slab") * lax.axis_size("sub")
-    start_gram = lax.psum(local_inner(start, start), ("slab", "sub")) / entry_count
+    start_gram = add_all(local_inner(start, start), ("slab", "sub")) / entry_count
     basis_block, upper_factor = normalize(start, start_gram)
     blocks = [basis_block]
     hessenberg = jnp.zeros((ITERS, ITERS + 1, rhs_count, rhs_count), jnp.float32)

time: 423 us -> 422 us (level)
    all_gather x0 -> x1, blocking collectives: none -> 44 us  [add_all(): pieces = lax.all_gather(x, axis, axis=0, tiled=False)]
    psum x1 -> x0, blocking collectives: 42 us -> none  [body(): lax.psum(local_inner(start, start), ('slab', 'sub')) / entry_count]
where the time goes in v1:
time: 422 us; the launch traced here: 421 us
  blocking collectives  234 us (55%)
  matrix products  61.1 us (14%)
  starting transfers between devices  43.3 us (10%)
  other arithmetic  33.8 us (8%)
  waiting for transfers between devices  24.5 us (6%)
  local copies, waits for them, and re-layouts  22.5 us (5%)
    psum x4, blocking collectives, body(): lax.psum((local_terms, local_inner(image_block, image_block)), ('slab', '...  190 us
    all_gather x1, blocking collectives, add_all(): pieces = lax.all_gather(x, axis, axis=0, tiled=False)  44 us
    ppermute x8, starting transfers between devices, extended(): before = lax.ppermute(last, axis, up)  32.9 us
    ppermute x8, waiting for transfers between devices, extended(): before = lax.ppermute(last, axis, up)  16.8 us
    dot_general x12, matrix products, complex_apply(): jnp.einsum(layout, matrix_real, vec_real, preferred_element_type=jnp.floa...  12.9 us
    dot_general x12, matrix products, complex_apply(): jnp.einsum(layout, matrix_real, vec_imag, preferred_element_type=jnp.floa...  11.8 us
    another operation x15, other arithmetic, normalize(): low_factor = jnp.linalg.cholesky(gram_matrix)  10.7 us
    ppermute x8, starting transfers between devices, extended(): after = lax.ppermute(leading, axis, down)  10.3 us
  transfers between devices with their start and end apart: 16, of which 11 were waited for; matrix products, arithmetic and copies ran while one was open for 1% of the time, Pallas kernels for 0%

profile of v1, /device:TPU:0, one launch (start us, length us, event | category | flops | bytes accessed | tf_op | source)
XLA Modules:
  0.0 421.0 jit_solution(3401171294624264121)
XLA Ops:
  2.8 2.1 gather_fusion
  5.0 1.9 copy.73
  7.2 44.0 %all-gather = f32[512,16]{1,0:T(8,128)S(1)} all-gather(f32[16,16]{1,0:T(8,128)S(1)} %convolution_bitcast_fusion.21), channel_id=2, replica_groups=mesh['slab'=8,'sub'=4] {'slab','sub'}, dimensions={0}, use_global_device_ids=true | all-gather | bytes 33792 | tf_op jit(solution)/shard_map/all_gather | solution.py:11
  51.4 1.5 cholesky.89
  57.4 2.0 fusion.119
  59.5 1.9 fusion.13
  61.3 1.9 fusion.12
  67.1 2.1 gather_fusion.1
  69.3 1.7 copy.76
  74.6 1.3 collective-permute-start.1
  75.9 4.6 %collective-permute-start = (f32[1,1,2,6,2,16,128]{6,5,4,3,2,1,0:T(8,128)S(1)}, f32[1,1,2,6,2,16,128]{6,5,4,3,2,1,0:T(8,128)S(1)}, u32[]{:S(2)}, u32[]{:S(2)}) collective-permute-start(f32[1,1,2,6,2,16,128]{6,5,4,3,2,1,0:T(8,128)S(1)} %fusion.108), channel_id=1, source_target_pairs={{0,4},{4,8},{8,12},{12,16},{16,20},{20,24},{24,28},{1,5},{5,9},{9,... | collective-permute-start | bytes 589832 | tf_op jit(solution)/shard_map/ppermute | solution.py:23
  80.5 3.2 collective-permute-done.1
  87.0 3.9 collective-permute-start.2
  92.0 2.7 pad_maximum_fusion
  94.7 2.0 gather_fusion.2
  97.6 46.6 %all-reduce.4 = (f32[16,16]{0,1:T(8,128)S(1)}, f32[1,16,16]{2,1,0:T(8,128)S(1)}) all-reduce(f32[16,16]{0,1:T(8,128)S(1)} %convolution_bitcast_fusion.20, f32[1,16,16]{2,1,0:T(8,128)S(1)} %convolution_bitcast_fusion.19), channel_id=1, replica_groups=mesh['slab'=8,'sub'=4] {'slab','sub'}, use_global_device_ids=true, to_apply=%region_3.7 | all-reduce | flops 512 | bytes 4096 | tf_op jit(solution)/shard_map/psum | solution.py:154
  144.8 1.5 cholesky.100
  150.7 2.0 fusion.116
  152.7 1.9 fusion.117
  164.8 4.8 %collective-permute-start.4 = (f32[1,1,2,6,2,16,128]{6,5,4,3,2,1,0:T(8,128)S(1)}, f32[1,1,2,6,2,16,128]{6,5,4,3,2,1,0:T(8,128)S(1)}, u32[]{:S(2)}, u32[]{:S(2)}) collective-permute-start(f32[1,1,2,6,2,16,128]{6,5,4,3,2,1,0:T(8,128)S(1)} %fusion.103), channel_id=1, source_target_pairs={{0,4},{4,8},{8,12},{12,16},{16,20},{20,24},{24,28},{1,5},{5,9},{9,... | collective-permute-start | bytes 589832 | tf_op jit(solution)/shard_map/ppermute | solution.py:23
  169.7 2.6 collective-permute-done.5
  172.3 4.4 %collective-permute-done.4 = f32[1,1,2,6,2,16,128]{6,5,4,3,2,1,0:T(8,128)S(1)} collective-permute-done((f32[1,1,2,6,2,16,128]{6,5,4,3,2,1,0:T(8,128)S(1)}, f32[1,1,2,6,2,16,128]{6,5,4,3,2,1,0:T(8,128)S(1)}, u32[]{:S(2)}, u32[]{:S(2)}) %collective-permute-start.4) | collective-permute-done | bytes 196640 | tf_op jit(solution)/shard_map/ppermute | solution.py:23
  178.0 3.1 collective-permute-start.6
  181.1 1.6 collective-permute-done.6
  182.6 1.4 pad_maximum_fusion.1
  184.0 2.0 gather_fusion.3
  187.0 47.7 %all-reduce.3 = (f32[2,16,16]{2,1,0:T(8,128)S(1)}, f32[16,16]{0,1:T(8,128)S(1)}) all-reduce(f32[2,16,16]{2,1,0:T(8,128)S(1)} %convolution_bitcast_fusion.7, f32[16,16]{0,1:T(8,128)S(1)} %convolution_bitcast_fusion.18), channel_id=1, replica_groups=mesh['slab'=8,'sub'=4] {'slab','sub'}, use_global_device_ids=true, to_apply=%region_6.10 | all-reduce | flops 768 | bytes 6144 | tf_op jit(solution)/shard_map/psum | solution.py:154
  235.4 1.5 cholesky.111
  241.3 2.0 fusion.114
  243.3 1.9 fusion.115
  254.1 1.3 collective-permute-start.9
  255.4 4.9 %collective-permute-start.8 = (f32[1,1,2,6,2,16,128]{6,5,4,3,2,1,0:T(8,128)S(1)}, f32[1,1,2,6,2,16,128]{6,5,4,3,2,1,0:T(8,128)S(1)}, u32[]{:S(2)}, u32[]{:S(2)}) collective-permute-start(f32[1,1,2,6,2,16,128]{6,5,4,3,2,1,0:T(8,128)S(1)} %fusion.101), channel_id=1, source_target_pairs={{0,4},{4,8},{8,12},{12,16},{16,20},{20,24},{24,28},{1,5},{5,9},{9,... | collective-permute-start | bytes 589832 | tf_op jit(solution)/shard_map/ppermute | solution.py:23
  260.2 1.7 collective-permute-done.9
  261.9 3.9 collective-permute-done.8
  265.9 1.3 collective-permute-start.11
  267.2 3.1 collective-permute-start.10
  271.9 1.4 pad_maximum_fusion.2
  273.3 2.0 gather_fusion.4
  276.4 49.0 %all-reduce.2 = (f32[3,16,16]{2,1,0:T(8,128)S(1)}, f32[16,16]{0,1:T(8,128)S(1)}) all-reduce(f32[3,16,16]{2,1,0:T(8,128)S(1)} %convolution_bitcast_fusion.6, f32[16,16]{0,1:T(8,128)S(1)} %convolution_bitcast_fusion.17), channel_id=1, replica_groups=mesh['slab'=8,'sub'=4] {'slab','sub'}, use_global_device_ids=true, to_apply=%region_8.12 | all-reduce | flops 1024 | bytes 8192 | tf_op jit(solution)/shard_map/psum | solution.py:154
  326.2 1.5 cholesky.122
  332.1 2.0 fusion.112
  334.1 1.9 fusion.113
  346.2 4.8 %collective-permute-start.12 = (f32[1,1,2,6,2,16,128]{6,5,4,3,2,1,0:T(8,128)S(1)}, f32[1,1,2,6,2,16,128]{6,5,4,3,2,1,0:T(8,128)S(1)}, u32[]{:S(2)}, u32[]{:S(2)}) collective-permute-start(f32[1,1,2,6,2,16,128]{6,5,4,3,2,1,0:T(8,128)S(1)} %fusion.99), channel_id=1, source_target_pairs={{0,4},{4,8},{8,12},{12,16},{16,20},{20,24},{24,28},{1,5},{5,9},{9,... | collective-permute-start | bytes 589832 | tf_op jit(solution)/shard_map/ppermute | solution.py:23
  352.8 3.8 collective-permute-done.12
  357.9 3.8 collective-permute-start.14
  363.4 1.4 pad_maximum_fusion.3
  366.6 47.0 %all-reduce.1 = (f32[4,16,16]{2,1,0:T(8,128)S(1)}, f32[16,16]{0,1:T(8,128)S(1)}) all-reduce(f32[4,16,16]{2,1,0:T(8,128)S(1)} %convolution_bitcast_fusion.5, f32[16,16]{0,1:T(8,128)S(1)} %convolution_bitcast_fusion.16), channel_id=1, replica_groups=mesh['slab'=8,'sub'=4] {'slab','sub'}, use_global_device_ids=true, to_apply=%region_10.14 | all-reduce | flops 1280 | bytes 10240 | tf_op jit(solution)/shard_map/psum | solution.py:154
  414.5 1.5 cholesky.133
  (237 shorter events, 81.7 us)
Async XLA Ops:
  0.6 2.2 copy-start
  5.0 1.9 copy-start.11
  6.9 49.9 %copy-start.2 = (bf16[32,2,128,128]{3,2,0,1:T(8,128)(2,1)}, bf16[32,2,128,128]{3,2,0,1:T(8,128)(2,1)S(1)}, u32[]{:S(2)}) copy-start(bf16[32,2,128,128]{3,2,0,1:T(8,128)(2,1)S(1)} %copy.73) | copy-start | bytes 6291460
  57.4 5.8 %copy-start.1 = (bf16[32,2,128,128]{3,2,1,0:T(8,128)(2,1)S(1)}, bf16[32,2,128,128]{3,2,1,0:T(8,128)(2,1)}, u32[]{:S(2)}) copy-start(bf16[32,2,128,128]{3,2,1,0:T(8,128)(2,1)} %param.34) | copy-start | bytes 6291460
  65.7 1.5 copy-start.10
  71.0 2.4 copy-start.6
  72.7 1.4 copy-start.21
  74.1 16.8 %copy-start.24 = (s32[2,6]{1,0:T(2,128)S(1)}, s32[2,6]{1,0:T(2,128)}, u32[]{:S(2)}) copy-start(s32[2,6]{1,0:T(2,128)} %param.36) | copy-start | bytes 148
  74.1 16.8 %copy-start.25 = (s32[2,6]{1,0:T(2,128)S(1)}, s32[2,6]{1,0:T(2,128)}, u32[]{:S(2)}) copy-start(s32[2,6]{1,0:T(2,128)} %param.35) | copy-start | bytes 148
  74.1 16.8 %copy-start.26 = (s32[6]{0:T(128)S(1)}, s32[6]{0:T(128)}, u32[]{:S(2)}) copy-start(s32[6]{0:T(128)} %constant.343) | copy-start | bytes 76
  74.6 9.0 %collective-permute-start.1 = (f32[1,1,2,6,2,16,128]{6,5,4,3,2,1,0:T(8,128)S(1)}, f32[1,1,2,6,2,16,128]{6,5,4,3,2,1,0:T(8,128)S(1)}, u32[]{:S(2)}, u32[]{:S(2)}) collective-permute-start(f32[1,1,2,6,2,16,128]{6,5,4,3,2,1,0:T(8,128)S(1)} %fusion.108), channel_id=1, source_target_pairs={{4,0},{8,4},{12,8},{16,12},{20,16},{24,20},{28,24},{5,1},{9,5},{13... | collective-permute-start | bytes 589832 | tf_op jit(solution)/shard_map/ppermute | solution.py:24
  75.9 8.9 %collective-permute-start = (f32[1,1,2,6,2,16,128]{6,5,4,3,2,1,0:T(8,128)S(1)}, f32[1,1,2,6,2,16,128]{6,5,4,3,2,1,0:T(8,128)S(1)}, u32[]{:S(2)}, u32[]{:S(2)}) collective-permute-start(f32[1,1,2,6,2,16,128]{6,5,4,3,2,1,0:T(8,128)S(1)} %fusion.108), channel_id=1, source_target_pairs={{0,4},{4,8},{8,12},{12,16},{16,20},{20,24},{24,28},{1,5},{5,9},{9,... | collective-permute-start | bytes 589832 | tf_op jit(solution)/shard_map/ppermute | solution.py:23
  85.7 5.3 %collective-permute-start.3 = (f32[3,1,2,6,2,16,128]{6,5,4,3,2,1,0:T(8,128)}, f32[3,1,2,6,2,16,128]{6,5,4,3,2,1,0:T(8,128)}, u32[]{:S(2)}, u32[]{:S(2)}) collective-permute-start(f32[3,1,2,6,2,16,128]{6,5,4,3,2,1,0:T(8,128)} %pad_maximum_fusion.5), channel_id=1, source_target_pairs={{1,0},{2,1},{3,2},{5,4},{6,5},{7,6},{9,8},{10,9},{11,10},{13,12},{... | collective-permute-start | bytes 1769480 | tf_op jit(solution)/shard_map/ppermute | solution.py:24
  87.0 5.0 %collective-permute-start.2 = (f32[3,1,2,6,2,16,128]{6,5,4,3,2,1,0:T(8,128)}, f32[3,1,2,6,2,16,128]{6,5,4,3,2,1,0:T(8,128)}, u32[]{:S(2)}, u32[]{:S(2)}) collective-permute-start(f32[3,1,2,6,2,16,128]{6,5,4,3,2,1,0:T(8,128)} %pad_maximum_fusion.5), channel_id=1, source_target_pairs={{0,1},{1,2},{2,3},{4,5},{5,6},{6,7},{8,9},{9,10},{10,11},{12,13},{... | collective-permute-start | bytes 1769480 | tf_op jit(solution)/shard_map/ppermute | solution.py:23
  91.0 184.3 %copy-start.22 = (pred[2,6]{1,0:T(4,128)(4,1)}, pred[2,6]{1,0:T(4,128)(4,1)S(1)}, u32[]{:S(2)}) copy-start(pred[2,6]{1,0:T(4,128)(4,1)S(1)} %broadcast_compare_fusion) | copy-start | bytes 40
  150.6 4.0 copy-start.3
  158.3 1.6 copy-start.7
  163.5 8.7 %collective-permute-start.5 = (f32[1,1,2,6,2,16,128]{6,5,4,3,2,1,0:T(8,128)S(1)}, f32[1,1,2,6,2,16,128]{6,5,4,3,2,1,0:T(8,128)S(1)}, u32[]{:S(2)}, u32[]{:S(2)}) collective-permute-start(f32[1,1,2,6,2,16,128]{6,5,4,3,2,1,0:T(8,128)S(1)} %fusion.103), channel_id=1, source_target_pairs={{4,0},{8,4},{12,8},{16,12},{20,16},{24,20},{28,24},{5,1},{9,5},{13... | collective-permute-start | bytes 589832 | tf_op jit(solution)/shard_map/ppermute | solution.py:24
  164.8 11.8 %collective-permute-start.4 = (f32[1,1,2,6,2,16,128]{6,5,4,3,2,1,0:T(8,128)S(1)}, f32[1,1,2,6,2,16,128]{6,5,4,3,2,1,0:T(8,128)S(1)}, u32[]{:S(2)}, u32[]{:S(2)}) collective-permute-start(f32[1,1,2,6,2,16,128]{6,5,4,3,2,1,0:T(8,128)S(1)} %fusion.103), channel_id=1, source_target_pairs={{0,4},{4,8},{8,12},{12,16},{16,20},{20,24},{24,28},{1,5},{5,9},{9,... | collective-permute-start | bytes 589832 | tf_op jit(solution)/shard_map/ppermute | solution.py:23
  176.7 4.4 %collective-permute-start.7 = (f32[3,1,2,6,2,16,128]{6,5,4,3,2,1,0:T(8,128)S(1)}, f32[3,1,2,6,2,16,128]{6,5,4,3,2,1,0:T(8,128)S(1)}, u32[]{:S(2)}, u32[]{:S(2)}) collective-permute-start(f32[3,1,2,6,2,16,128]{6,5,4,3,2,1,0:T(8,128)S(1)} %pad_maximum_fusion.6), channel_id=1, source_target_pairs={{1,0},{2,1},{3,2},{5,4},{6,5},{7,6},{9,8},{10,9},{11,10},{13,12},{... | collective-permute-start | bytes 1769480 | tf_op jit(solution)/shard_map/ppermute | solution.py:24
  178.0 4.7 %collective-permute-start.6 = (f32[3,1,2,6,2,16,128]{6,5,4,3,2,1,0:T(8,128)S(1)}, f32[3,1,2,6,2,16,128]{6,5,4,3,2,1,0:T(8,128)S(1)}, u32[]{:S(2)}, u32[]{:S(2)}) collective-permute-start(f32[3,1,2,6,2,16,128]{6,5,4,3,2,1,0:T(8,128)S(1)} %pad_maximum_fusion.6), channel_id=1, source_target_pairs={{0,1},{1,2},{2,3},{4,5},{5,6},{6,7},{8,9},{9,10},{10,11},{12,13},{... | collective-permute-start | bytes 1769480 | tf_op jit(solution)/shard_map/ppermute | solution.py:23
  234.7 5.3 %copy-start.16 = (f32[2,16,16]{2,1,0:T(8,128)}, f32[2,16,16]{2,1,0:T(8,128)S(1)}, u32[]{:S(2)}) copy-start(f32[2,16,16]{2,1,0:T(8,128)S(1)} %get-tuple-element.105) | copy-start | bytes 6148
  241.2 4.0 copy-start.4
  248.9 1.6 copy-start.8
  254.1 7.9 %collective-permute-start.9 = (f32[1,1,2,6,2,16,128]{6,5,4,3,2,1,0:T(8,128)S(1)}, f32[1,1,2,6,2,16,128]{6,5,4,3,2,1,0:T(8,128)S(1)}, u32[]{:S(2)}, u32[]{:S(2)}) collective-permute-start(f32[1,1,2,6,2,16,128]{6,5,4,3,2,1,0:T(8,128)S(1)} %fusion.101), channel_id=1, source_target_pairs={{4,0},{8,4},{12,8},{16,12},{20,16},{24,20},{28,24},{5,1},{9,5},{13... | collective-permute-start | bytes 589832 | tf_op jit(solution)/shard_map/ppermute | solution.py:24
  255.4 10.5 %collective-permute-start.8 = (f32[1,1,2,6,2,16,128]{6,5,4,3,2,1,0:T(8,128)S(1)}, f32[1,1,2,6,2,16,128]{6,5,4,3,2,1,0:T(8,128)S(1)}, u32[]{:S(2)}, u32[]{:S(2)}) collective-permute-start(f32[1,1,2,6,2,16,128]{6,5,4,3,2,1,0:T(8,128)S(1)} %fusion.101), channel_id=1, source_target_pairs={{0,4},{4,8},{8,12},{12,16},{16,20},{20,24},{24,28},{1,5},{5,9},{9,... | collective-permute-start | bytes 589832 | tf_op jit(solution)/shard_map/ppermute | solution.py:23
  265.9 5.0 %collective-permute-start.11 = (f32[3,1,2,6,2,16,128]{6,5,4,3,2,1,0:T(8,128)S(1)}, f32[3,1,2,6,2,16,128]{6,5,4,3,2,1,0:T(8,128)S(1)}, u32[]{:S(2)}, u32[]{:S(2)}) collective-permute-start(f32[3,1,2,6,2,16,128]{6,5,4,3,2,1,0:T(8,128)S(1)} %pad_maximum_fusion.7), channel_id=1, source_target_pairs={{1,0},{2,1},{3,2},{5,4},{6,5},{7,6},{9,8},{10,9},{11,10},{13,12},{... | collective-permute-start | bytes 1769480 | tf_op jit(solution)/shard_map/ppermute | solution.py:24
  267.2 4.7 %collective-permute-start.10 = (f32[3,1,2,6,2,16,128]{6,5,4,3,2,1,0:T(8,128)S(1)}, f32[3,1,2,6,2,16,128]{6,5,4,3,2,1,0:T(8,128)S(1)}, u32[]{:S(2)}, u32[]{:S(2)}) collective-permute-start(f32[3,1,2,6,2,16,128]{6,5,4,3,2,1,0:T(8,128)S(1)} %pad_maximum_fusion.7), channel_id=1, source_target_pairs={{0,1},{1,2},{2,3},{4,5},{5,6},{6,7},{8,9},{9,10},{10,11},{12,13},{... | collective-permute-start | bytes 1769480 | tf_op jit(solution)/shard_map/ppermute | solution.py:23
  325.4 5.4 %copy-start.14 = (f32[3,16,16]{2,1,0:T(8,128)}, f32[3,16,16]{2,1,0:T(8,128)S(1)}, u32[]{:S(2)}) copy-start(f32[3,16,16]{2,1,0:T(8,128)S(1)} %get-tuple-element.103) | copy-start | bytes 9220
  332.0 4.0 copy-start.5
  339.7 1.6 copy-start.9
  343.7 7.4 %copy-start.18 = (f32[1,1,16,16]{2,3,1,0:T(8,128)S(1)}, f32[1,1,16,16]{2,3,1,0:T(8,128)}, u32[]{:S(2)}) copy-start(f32[1,1,16,16]{2,3,1,0:T(8,128)} %get-tuple-element.115) | copy-start | bytes 3076
  343.7 8.7 %copy-start.19 = (f32[1,1,16,16]{2,3,1,0:T(8,128)S(1)}, f32[1,1,16,16]{2,3,1,0:T(8,128)}, u32[]{:S(2)}) copy-start(f32[1,1,16,16]{2,3,1,0:T(8,128)} %get-tuple-element.113) | copy-start | bytes 3076
  344.4 17.4 %copy-start.17 = (f32[2,16,16]{2,1,0:T(8,128)S(1)}, f32[2,16,16]{2,1,0:T(8,128)}, u32[]{:S(2)}) copy-start(f32[2,16,16]{2,1,0:T(8,128)} %copy-done.16) | copy-start | bytes 6148
  344.4 17.4 %copy-start.20 = (f32[1,1,16,16]{2,3,1,0:T(8,128)S(1)}, f32[1,1,16,16]{2,3,1,0:T(8,128)}, u32[]{:S(2)}) copy-start(f32[1,1,16,16]{2,3,1,0:T(8,128)} %get-tuple-element.111) | copy-start | bytes 3076
  344.4 17.5 %copy-start.15 = (f32[3,16,16]{2,1,0:T(8,128)S(1)}, f32[3,16,16]{2,1,0:T(8,128)}, u32[]{:S(2)}) copy-start(f32[3,16,16]{2,1,0:T(8,128)} %copy-done.14) | copy-start | bytes 9220
  344.9 7.8 %collective-permute-start.13 = (f32[1,1,2,6,2,16,128]{6,5,4,3,2,1,0:T(8,128)S(1)}, f32[1,1,2,6,2,16,128]{6,5,4,3,2,1,0:T(8,128)S(1)}, u32[]{:S(2)}, u32[]{:S(2)}) collective-permute-start(f32[1,1,2,6,2,16,128]{6,5,4,3,2,1,0:T(8,128)S(1)} %fusion.99), channel_id=1, source_target_pairs={{4,0},{8,4},{12,8},{16,12},{20,16},{24,20},{28,24},{5,1},{9,5},{13... | collective-permute-start | bytes 589832 | tf_op jit(solution)/shard_map/ppermute | solution.py:24
  346.2 10.3 %collective-permute-start.12 = (f32[1,1,2,6,2,16,128]{6,5,4,3,2,1,0:T(8,128)S(1)}, f32[1,1,2,6,2,16,128]{6,5,4,3,2,1,0:T(8,128)S(1)}, u32[]{:S(2)}, u32[]{:S(2)}) collective-permute-start(f32[1,1,2,6,2,16,128]{6,5,4,3,2,1,0:T(8,128)S(1)} %fusion.99), channel_id=1, source_target_pairs={{0,4},{4,8},{8,12},{12,16},{16,20},{20,24},{24,28},{1,5},{5,9},{9,... | collective-permute-start | bytes 589832 | tf_op jit(solution)/shard_map/ppermute | solution.py:23
  356.6 8.8 %copy-start.23 = (pred[2,6]{1,0:T(4,128)(4,1)S(1)}, pred[2,6]{1,0:T(4,128)(4,1)}, u32[]{:S(2)}) copy-start(pred[2,6]{1,0:T(4,128)(4,1)} %copy-done.22) | copy-start | bytes 40
  356.6 5.3 %collective-permute-start.15 = (f32[3,1,2,6,2,16,128]{6,5,4,3,2,1,0:T(8,128)S(1)}, f32[3,1,2,6,2,16,128]{6,5,4,3,2,1,0:T(8,128)S(1)}, u32[]{:S(2)}, u32[]{:S(2)}) collective-permute-start(f32[3,1,2,6,2,16,128]{6,5,4,3,2,1,0:T(8,128)S(1)} %pad_maximum_fusion.9), channel_id=1, source_target_pairs={{1,0},{2,1},{3,2},{5,4},{6,5},{7,6},{9,8},{10,9},{11,10},{13,12},{... | collective-permute-start | bytes 1769480 | tf_op jit(solution)/shard_map/ppermute | solution.py:24
  357.9 5.4 %collective-permute-start.14 = (f32[3,1,2,6,2,16,128]{6,5,4,3,2,1,0:T(8,128)S(1)}, f32[3,1,2,6,2,16,128]{6,5,4,3,2,1,0:T(8,128)}, u32[]{:S(2)}, u32[]{:S(2)}) collective-permute-start(f32[3,1,2,6,2,16,128]{6,5,4,3,2,1,0:T(8,128)S(1)} %pad_maximum_fusion.9), channel_id=1, source_target_pairs={{0,1},{1,2},{2,3},{4,5},{5,6},{6,7},{8,9},{9,10},{10,11},{12,13},{... | collective-permute-start | bytes 1769480 | tf_op jit(solution)/shard_map/ppermute | solution.py:23
  361.9 0.7 copy-start.13
  362.6 0.8 copy-start.12
